TPU v7x, 256 devices: a whole 4x4x8 slice. The times are simulated.
256 devices in a mesh: tm: 8 (over z_hi, x), chan: 32 (over z_lo, y, core).
Axes of the slice: x: 4, y: 4, z: 8 (z_hi: 2, z_lo: 4; z = z_hi * 4 + z_lo), core: 2. Of those that a mesh axis runs over, the one named last changes fastest.
Arguments:
- voltage_frequency_samples: bfloat16 [2, 256, 30, 2, 8192], P(None, ('tm', 'chan')), may hold values from -6 to 6
- lag_lookup_entry: int32 [8, 8, 30], P('tm'), may hold values from 0 to 63
- lag_lookup_turning: float32 [64, 8192], P(None, 'chan'), may hold values from -3.140625 to 3.140625
- antenna_pair_members: int32 [435, 2], replicated, may hold values from 0 to 29, as said below
- frequency_bin_target: int32 [8192], P('chan'), may hold values from 0 to 63, as said below
Outputs:
- centre_vis: float32 [512, 2, 4, 435], P(('tm', 'chan'))
Inputs may be any that keep to these rules, and one draw needn't show every extreme that they name: `antenna_pair_members`: every unordered pair of two different stations of the 30 appears in exactly one row, in either order. `frequency_bin_target`: each of the 64 output channels receives exactly 128 fine channels.
All inputs are finite; a program needn't handle non-finite values.
Results may differ from a plain program's by a relative error of at most 0.0029.
Values may be sent and summed in bfloat16 or wider, within the bound.
A program may use at most 128 MiB of HBM per device.

v0:
```python
import jax
import jax.numpy as jnp
from jax import lax
from jax.sharding import PartitionSpec as P

F = 8192
Q = 64
G_DEV = 1


def correlate(left_part, right_part):
    return jnp.einsum("gtaf,gtbf->gabf", left_part, right_part, preferred_element_type=jnp.float32)


def on_device(
    voltage_frequency_samples,
    lag_lookup_entry,
    lag_lookup_turning,
    antenna_pair_members,
    frequency_bin_target,
):
    regrouped = lax.all_to_all(
        voltage_frequency_samples, "chan", split_axis=4, concat_axis=1, tiled=True
    )
    fine_local = regrouped.shape[4]
    selector = (frequency_bin_target[:, None] == jnp.arange(Q, dtype=jnp.int32)[None, :]).astype(
        jnp.bfloat16
    )
    spectra_count = regrouped.shape[1]
    stations = regrouped.shape[2]
    polars = regrouped.shape[3]
    antenna_pair_total = antenna_pair_members.shape[0]
    shaped = regrouped.reshape(2, G_DEV, spectra_count // G_DEV, stations * polars, fine_local)
    real_part = shaped[0]
    imag_part = shaped[1]
    vis_real = correlate(real_part, real_part) + correlate(imag_part, imag_part)
    vis_imag = correlate(imag_part, real_part) - correlate(real_part, imag_part)
    left_antenna_number = antenna_pair_members[:, 0]
    right_antenna_number = antenna_pair_members[:, 1]
    full_shape = (G_DEV, stations, polars, stations, polars, fine_local)
    picked_real = vis_real.reshape(full_shape)[:, left_antenna_number, :, right_antenna_number]
    picked_imag = vis_imag.reshape(full_shape)[:, left_antenna_number, :, right_antenna_number]
    base_real = jnp.transpose(picked_real, (1, 2, 3, 0, 4)).reshape(
        G_DEV, polars * polars, antenna_pair_total, fine_local
    )
    base_imag = jnp.transpose(picked_imag, (1, 2, 3, 0, 4)).reshape(
        G_DEV, polars * polars, antenna_pair_total, fine_local
    )
    station_phase = jnp.take(lag_lookup_turning, lag_lookup_entry, axis=0)
    phase_diff = (
        station_phase[:, :, left_antenna_number] - station_phase[:, :, right_antenna_number]
    )
    cosine = jnp.cos(phase_diff)
    sine = jnp.sin(phase_diff)
    centres = lag_lookup_entry.shape[1]
    partial_list = []
    for centre in range(centres):
        cos_now = cosine[:, centre][:, None]
        sin_now = sine[:, centre][:, None]
        rot_real = (base_real * cos_now + base_imag * sin_now).astype(jnp.bfloat16)
        rot_imag = (base_imag * cos_now - base_real * sin_now).astype(jnp.bfloat16)
        rotated = jnp.stack([rot_real, rot_imag])
        partial_list.append(
            jnp.einsum("rgpbf,fq->qrpb", rotated, selector, preferred_element_type=jnp.float32)
        )
    partial_value = jnp.stack(partial_list)
    columns = selector.shape[1]
    tail = (2, polars * polars, antenna_pair_total)
    flat = partial_value.reshape((centres * columns,) + tail)
    channel_summed_products = lax.psum_scatter(
        flat, ("tm", "chan"), scatter_dimension=0, tiled=True
    )
    return channel_summed_products * (Q / F)


def solution(mesh):
    return jax.shard_map(
        on_device,
        mesh=mesh,
        in_specs=(
            P(None, ("tm", "chan"), None, None, None),
            P("tm", None, None),
            P(None, "chan"),
            P(),
            P("chan"),
        ),
        out_specs=P(("tm", "chan"), None, None, None),
        check_vma=False,
    )
```

profile of v0, /device:TPU:24, one launch (start us, length us, event | category | flops | bytes accessed | tf_op | source)
XLA Modules:
  0.0 533.8 jit_solution(12457336647658863745)
XLA Ops:
  6.5 19.7 %copy.43 = bf16[2,1,30,2,8192]{2,3,1,0,4:T(2,128)(2,1)} copy(bf16[2,1,30,2,8192]{4,3,2,1,0:T(2,128)(2,1)} %param.5) | data formatting | bytes 3932160 | tf_op args[0]
  26.2 17.3 %reshape.729 = bf16[32,2,15360]{2,1,0:T(2,128)(2,1)} reshape(bf16[8192,2,1,2,30]{4,3,2,1,0:T(2,128)(2,1)} %bitcast.325) | data formatting | bytes 3932160
  43.5 9.0 %all-to-all-start = ((bf16[32,2,15360]{2,1,0:T(2,128)(2,1)}), bf16[32,2,15360]{2,1,0:T(2,128)(2,1)S(1)}, u32[]{:S(2)}, u32[]{:S(2)}) async-start(bf16[32,2,15360]{2,1,0:T(2,128)(2,1)} %reshape.729), calls=%async_computation | async-start | bytes 3932160 | tf_op jit(solution)/shard_map/all_to_all | solution.py:22
  53.0 0.9 gather_fusion.1
  54.3 2.9 gather_fusion.2
  57.2 2.9 gather_fusion.3
  60.1 13.8 %cosine_bitcast_fusion = (f32[1,8,435,256]{3,1,2,0:T(8,128)S(1)}, f32[1,8,435,256]{3,1,2,0:T(8,128)S(1)}) fusion(f32[435,8,256]{2,1,0:T(8,128)} %gather_fusion.2, f32[435,8,256]{2,1,0:T(8,128)} %gather_fusion.3), kind=kLoop, calls=%fused_computation.8 | loop fusion | flops 890880 | bytes 14254080 | tf_op jit(solution)/shard_map/cos | solution.py:53
  74.0 2.4 fusion.99
  76.4 0.8 copy.98
  77.2 2.4 fusion.98
  79.6 0.8 copy.99
  80.4 0.8 copy.100
  81.3 0.9 copy.101
  82.1 0.8 copy.102
  82.9 0.8 copy.103
  83.7 0.8 copy.104
  84.5 0.8 copy.105
  85.4 0.8 copy.106
  87.0 0.8 copy.108
  87.8 0.8 copy.109
  88.6 0.8 copy.110
  89.4 0.8 copy.111
  90.2 0.8 copy.112
  91.0 0.8 copy.113
  91.8 6.4 %all-to-all-done = bf16[32,2,15360]{2,1,0:T(2,128)(2,1)S(1)} async-done(((bf16[32,2,15360]{2,1,0:T(2,128)(2,1)}), bf16[32,2,15360]{2,1,0:T(2,128)(2,1)S(1)}, u32[]{:S(2)}, u32[]{:S(2)}) %all-to-all-start) | async-done | bytes 1966112 | tf_op jit(solution)/shard_map/all_to_all | solution.py:22
  98.2 24.0 %reshape.730 = bf16[8192,2,1,2,30]{4,3,2,1,0:T(2,128)(2,1)} reshape(bf16[32,2,15360]{2,1,0:T(2,128)(2,1)S(1)} %all-to-all-done) | data formatting | bytes 3932160
  122.2 12.3 %copy.62 = bf16[2,1,30,2,32,256]{5,4,3,2,1,0:T(8,128)(2,1)S(1)} copy(bf16[2,1,30,2,32,256]{2,3,0,5,4,1:T(2,128)(2,1)} %bitcast.324) | data formatting | bytes 3932160 | tf_op jit(solution)/shard_map/all_to_all | solution.py:22
  134.5 1.2 fusion.100
  135.7 5.3 copy.45
  141.0 4.2 copy.47
  145.1 6.9 %fusion.101 = f32[256,60,60]{2,1,0:T(8,128)} fusion(bf16[32,60,256]{1,0,2:T(8,128)(2,1)} %copy.45), kind=kOutput, calls=%fused_computation.169 | convolution fusion | flops 58982400 | bytes 4669440 | tf_op jit(solution)/shard_map/gtaf,gtbf->gabf/dot_general | solution.py:12
  152.1 1.3 fusion.102
  153.4 4.6 subtract_bitcast_fusion
  158.0 8.6 %copy.57 = f32[1,60,60,256]{3,2,1,0:T(8,128)} copy(f32[1,60,60,256]{1,2,3,0:T(8,128)} %subtract_bitcast_fusion) | data formatting | bytes 7372800 | tf_op jit(solution)/shard_map/sub | solution.py:37
  166.6 5.6 %reshape.712 = f32[30,2,30,2,256]{4,3,2,1,0:T(2,128)} reshape(f32[1,60,60,256]{3,2,1,0:T(8,128)} %copy.57) | data formatting | bytes 7372800 | tf_op jit(solution)/shard_map/reshape | solution.py:42
  172.2 8.1 %gather_fusion.4 = f32[435,2,2,256]{3,2,1,0:T(2,128)} fusion(f32[30,2,30,2,256]{4,3,2,1,0:T(2,128)} %reshape.712, s32[435]{0:T(512)S(1)} %bitcast.322), kind=kCustom, calls=%fused_computation.4 | custom fusion | bytes 3567000 | tf_op jit(solution)/shard_map/gather | solution.py:42
  180.3 3.1 copy.58
  183.4 7.9 %add_bitcast_fusion = f32[1,60,60,256]{1,2,3,0:T(8,128)} fusion(f32[256,60,60]{2,1,0:T(8,128)} %fusion.101, bf16[32,60,256]{1,0,2:T(8,128)(2,1)S(1)} %copy.47), kind=kOutput, calls=%fused_computation.6 | convolution fusion | flops 59904000 | bytes 8355840 | tf_op jit(solution)/shard_map/gtaf,gtbf->gabf/dot_general | solution.py:12
  191.3 8.6 %copy.49 = f32[1,60,60,256]{3,2,1,0:T(8,128)} copy(f32[1,60,60,256]{1,2,3,0:T(8,128)} %add_bitcast_fusion) | data formatting | bytes 7372800 | tf_op jit(solution)/shard_map/add | solution.py:36
  199.9 5.6 %reshape.676 = f32[30,2,30,2,256]{4,3,2,1,0:T(2,128)} reshape(f32[1,60,60,256]{3,2,1,0:T(8,128)} %copy.49) | data formatting | bytes 7372800 | tf_op jit(solution)/shard_map/reshape | solution.py:41
  205.6 7.0 %gather_fusion = f32[435,2,2,256]{3,2,1,0:T(2,128)S(1)} fusion(f32[30,2,30,2,256]{4,3,2,1,0:T(2,128)} %reshape.676, s32[435]{0:T(512)S(1)} %bitcast.323), kind=kCustom, calls=%fused_computation | custom fusion | bytes 3567000 | tf_op jit(solution)/shard_map/gather | solution.py:41
  213.0 1.1 copy-done.3
  214.6 7.7 %fusion.53 = (bf16[1,1,4,435,256]{4,3,2,0,1:T(8,128)(2,1)S(1)}, bf16[1,1,4,435,256]{4,3,2,0,1:T(8,128)(2,1)S(1)}, bf16[1,1,4,435,256]{4,3,2,0,1:T(8,128)(2,1)S(1...) fusion(f32[1,2,2,435,256]{4,3,2,1,0:T(8,128)S(1)} %copy-done.3,, ...), kind=kLoop, calls=%fused_computation.86 | loop fusion | flops 28508160 | bytes 24944640 | tf_op jit(solution)/shard_map/convert_element_type | solution.py:60
  222.3 2.2 fusion.71
  228.9 4.3 copy.59
  233.2 12.0 %copy.60 = f32[512,2,4,435]{3,2,1,0:T(4,128)} copy(f32[512,2,4,435]{3,0,2,1:T(8,128)} %bitcast.326) | data formatting | bytes 14254080 | tf_op jit(solution)/shard_map/reshape | solution.py:69
  245.3 280.1 %all-reduce.3.cloned.1.call-done = f32[512,2,4,435]{3,2,1,0:T(4,128)} async-done(((f32[512,2,4,435]{3,2,1,0:T(4,128)}), f32[512,2,4,435]{3,2,1,0:T(4,128)}) %all-reduce.3.cloned.1.call-update) | async-done | bytes 7127056
  525.3 1.4 dynamic-slice_multiply_fusion
  (49 shorter events, 6.9 us)
Async XLA Ops:
  6.5 46.5 %copy-start = (f32[64,256]{1,0:T(8,128)S(1)}, f32[64,256]{1,0:T(8,128)}, u32[]{:S(2)}) copy-start(f32[64,256]{1,0:T(8,128)} %param.7) | copy-start | bytes 196612
  43.5 9.4 %copy-start.12 = (s32[1,8,30]{2,1,0:T(8,128)S(1)}, s32[1,8,30]{2,1,0:T(8,128)}, u32[]{:S(2)}) copy-start(s32[1,8,30]{2,1,0:T(8,128)} %param.6) | copy-start | bytes 2884
  43.5 54.7 %all-to-all-start = ((bf16[32,2,15360]{2,1,0:T(2,128)(2,1)}), bf16[32,2,15360]{2,1,0:T(2,128)(2,1)S(1)}, u32[]{:S(2)}, u32[]{:S(2)}) async-start(bf16[32,2,15360]{2,1,0:T(2,128)(2,1)} %reshape.729), calls=%async_computation | async-start | bytes 3932160 | tf_op jit(solution)/shard_map/all_to_all | solution.py:22
  52.6 1.6 copy-start.13
  52.6 472.8 %all-reduce.3.cloned.1.call-start = ((), (), s32[]{:S(2)}) async-start(), calls=%async_computation.1 | async-start | bytes 16777216
  145.1 6.9 %copy-start.2 = (bf16[32,60,256]{1,0,2:T(8,128)(2,1)S(1)}, bf16[32,60,256]{1,0,2:T(8,128)(2,1)}, u32[]{:S(2)}) copy-start(bf16[32,60,256]{1,0,2:T(8,128)(2,1)} %copy.45) | copy-start | bytes 2949124
  205.6 7.4 %copy-start.8 = (f32[1,1,435,256]{3,2,1,0:T(8,128)S(1)}, f32[1,1,435,256]{3,2,1,0:T(8,128)}, u32[]{:S(2)}) copy-start(f32[1,1,435,256]{3,2,1,0:T(8,128)} %copy.102) | copy-start | bytes 1336324
  205.6 7.4 %copy-start.9 = (f32[1,1,435,256]{3,2,1,0:T(8,128)S(1)}, f32[1,1,435,256]{3,2,1,0:T(8,128)}, u32[]{:S(2)}) copy-start(f32[1,1,435,256]{3,2,1,0:T(8,128)} %copy.103) | copy-start | bytes 1336324
  205.6 7.4 %copy-start.10 = (f32[1,1,435,256]{3,2,1,0:T(8,128)S(1)}, f32[1,1,435,256]{3,2,1,0:T(8,128)}, u32[]{:S(2)}) copy-start(f32[1,1,435,256]{3,2,1,0:T(8,128)} %copy.104) | copy-start | bytes 1336324
  212.6 1.5 copy-start.3
  212.6 1.5 copy-start.4
  212.6 1.7 copy-start.5
  212.6 1.8 copy-start.6
  212.6 1.9 copy-start.7
  214.6 7.7 %copy-start.14 = (s32[256]{0:T(256)S(1)}, s32[256]{0:T(256)}, u32[]{:S(2)}) copy-start(s32[256]{0:T(256)} %param.9) | copy-start | bytes 3076
  222.2 2.2 copy-start.11
  245.3 281.5 %copy-start.1 = (f32[64,256]{1,0:T(8,128)S(1)}, f32[64,256]{1,0:T(8,128)}, u32[]{:S(2)}) copy-start(f32[64,256]{1,0:T(8,128)} %param.7) | copy-start | bytes 196612
Sparse Core Ops, SparseCore 0:
  245.4 279.9 all-reduce.2
where the time goes:
time: 539 us; the launch traced here: 534 us
  waiting for transfers between devices  286 us (53%)
  local copies, waits for them, and re-layouts  173 us (32%)
  matrix products  27.4 us (5%)
  other arithmetic  23.1 us (4%)
  between operations  14 us (3%)
  starting transfers between devices  9.37 us (2%)
    unnamed x2, waiting for transfers between devices  280 us
    unnamed x49, local copies, waits for them, and re-layouts  75.5 us
    dot_general x4, matrix products, correlate(): jnp.einsum('gtaf,gtbf->gabf', left_part, right_part, preferred_element_ty...  20.8 us
    cos x1, other arithmetic, on_device(): cosine = jnp.cos(phase_diff)  13.8 us
    all_to_all x1, local copies, waits for them, and re-layouts, on_device(): lax.all_to_all(voltage_frequency_samples, 'chan', split_axis=4, concat_ax...  12.3 us
    reshape x1, local copies, waits for them, and re-layouts, on_device(): flat = partial_value.reshape((centres * columns,) + tail)  12 us
  transfers between devices with their start and end apart: 2, of which 2 were waited for; matrix products, arithmetic and copies ran while one was open for 7% of the time, Pallas kernels for 0%

commit v1 on v0

v1 whole, which is shorter than its diff:
```python
import functools

import jax
import jax.numpy as jnp
from jax import lax
from jax.experimental import pallas as pl
from jax.experimental.pallas import tpu as pltpu
from jax.sharding import PartitionSpec as P

F = 8192
Q = 64
S = 30
SP = 60
C = 8
K = 64
B = 435
OWN = 4096
STEP = 8192.0
MESH = pl.DeviceIdType.MESH
BF = jnp.bfloat16
F32 = jnp.float32


def place():
    tm = lax.axis_index("tm")
    ch = lax.axis_index("chan")
    return tm % 4, (ch // 2) % 4, (tm // 4) * 4 + ch // 8, ch % 2


def device(x, y, z, core):
    x, y, z = lax.rem(x + 4, 4), lax.rem(y + 4, 4), lax.rem(z + 8, 8)
    return ((z // 4) * 4 + x, (z % 4) * 8 + y * 2 + core)


def nt(a, b):
    return lax.dot_general(a, b, (((1,), (1,)), ((), ())), preferred_element_type=F32)


def gather_kernel(sh_ref, v_ref, full_ref, vp_ref, lsem, own_s, y_s, z_s, c_s, rsem, crsem, vsem):
    x, y, z, core = place()
    zl = z % 4
    partner = device(x, y, z, 1 - core)
    y_peers = [device(x, y + d, z, core) for d in (1, 2, 3)]
    z_peers = [device(x, y, z + d, core) for d in (1, 7, 2, 6)]
    barrier = pltpu.get_barrier_semaphore()
    for peer in [partner] + y_peers + z_peers:
        pl.semaphore_signal(barrier, inc=1, device_id=peer, device_id_type=MESH)
    pl.semaphore_wait(barrier, 8)

    vcopy = pltpu.make_async_remote_copy(
        src_ref=v_ref, dst_ref=vp_ref, send_sem=vsem.at[0], recv_sem=vsem.at[1],
        device_id=partner, device_id_type=MESH,
    )
    vcopy.start()

    def slot(zs, ys):
        return full_ref.at[core, zs, ys]

    def push(src, zs, ys, send, recv, peer):
        copy = pltpu.make_async_remote_copy(
            src_ref=src, dst_ref=slot(zs, ys), send_sem=send, recv_sem=recv,
            device_id=peer, device_id_type=MESH,
        )
        copy.start()
        return copy

    sent = []
    own = pltpu.make_async_copy(sh_ref, slot(zl, y), lsem)
    own.start()
    for n, peer in enumerate(y_peers):
        sent.append(push(sh_ref, zl, y, own_s.at[n], rsem.at[zl * 4 + y], peer))

    def spread(dy, src):
        ys = lax.rem(y + dy, 4)
        far = device(x, y, z + 2 + 4 * (ys % 2), core)
        for n, peer in enumerate([z_peers[0], z_peers[1], far]):
            sent.append(push(src, zl, ys, z_s.at[dy, n], rsem.at[zl * 4 + ys], peer))
        sent.append(push(src, zl, ys, c_s.at[0, dy], crsem.at[zl * 4 + ys], partner))

    def arrive(zs, ys):
        pltpu.make_async_remote_copy(
            src_ref=slot(zs, ys), dst_ref=slot(zs, ys), send_sem=lsem, recv_sem=rsem.at[zs * 4 + ys],
            device_id=partner, device_id_type=MESH,
        ).wait_recv()

    spread(0, sh_ref)
    for dy in (1, 3, 2):
        ys = lax.rem(y + dy, 4)
        arrive(zl, ys)
        spread(dy, slot(zl, ys))
    for dz in (1, 3, 2):
        zs = lax.rem(zl + dz, 4)
        for dy in (0, 1, 3, 2):
            ys = lax.rem(y + dy, 4)
            arrive(zs, ys)
            sent.append(push(slot(zs, ys), zs, ys, c_s.at[dz, dy], crsem.at[zs * 4 + ys], partner))
    for zs in range(4):
        for ys in range(4):
            other = full_ref.at[1 - core, zs, ys]
            pltpu.make_async_remote_copy(
                src_ref=other, dst_ref=other, send_sem=lsem, recv_sem=crsem.at[zs * 4 + ys],
                device_id=partner, device_id_type=MESH,
            ).wait_recv()
    for copy in sent:
        copy.wait_send()
    own.wait()
    vcopy.wait()


def gather(shard, volts):
    return pl.pallas_call(
        gather_kernel,
        out_shape=(
            jax.ShapeDtypeStruct((2, 4, 4) + shard.shape, shard.dtype),
            jax.ShapeDtypeStruct(volts.shape, volts.dtype),
        ),
        in_specs=[pl.BlockSpec(memory_space=pltpu.VMEM), pl.BlockSpec(memory_space=pl.ANY)],
        out_specs=(pl.BlockSpec(memory_space=pl.ANY), pl.BlockSpec(memory_space=pl.ANY)),
        scratch_shapes=[
            pltpu.SemaphoreType.DMA,
            pltpu.SemaphoreType.DMA((3,)),
            pltpu.SemaphoreType.DMA((1,)),
            pltpu.SemaphoreType.DMA((4, 3)),
            pltpu.SemaphoreType.DMA((4, 4)),
            pltpu.SemaphoreType.DMA((16,)),
            pltpu.SemaphoreType.DMA((16,)),
            pltpu.SemaphoreType.DMA((2,)),
        ],
        compiler_params=pltpu.CompilerParams(collective_id=0, has_side_effects=True),
        name="gather",
    )(shard, volts)


def sin_cos(phase):
    h = phase * 0.5
    u = h * h
    s = h * (1.0 + u * (-1.6666666666666666e-1 + u * (8.3333333333333332e-3 + u * (
        -1.9841269841269841e-4 + u * (2.7557319223985893e-6 + u * (-2.5052108385441720e-8 + u * 1.6059043836821613e-10))))))
    c = 1.0 + u * (-0.5 + u * (4.1666666666666664e-2 + u * (-1.3888888888888889e-3 + u * (
        2.4801587301587302e-5 + u * (-2.7557319223985888e-7 + u * (2.0876756987868100e-9 + u * -1.1470745597729725e-11))))))
    return 2.0 * s * c, 1.0 - 2.0 * s * s


def halves(value):
    hi = value.astype(BF)
    return hi, (value - hi.astype(F32)).astype(BF)


def local_kernel(va_ref, vb_ref, full_ref, pick_ref, ax_ref, by_ref, grid_ref, sorted_ref, perm_ref, perm_smem, cs_ref, sem):
    core = lax.axis_index("chan") % 2
    lane = lambda r, c: lax.broadcasted_iota(jnp.int32, (r, c), 1)
    row = lambda r, c: lax.broadcasted_iota(jnp.int32, (r, c), 0)

    kk = row(32, 1)
    bin_of = 4 * (kk // 2) + 2 * core + kk % 2
    before = (row(256, 256) < lane(256, 256)).astype(BF)
    fine = lane(1, 256).astype(F32)

    def rank_step(n, carry):
        base, high, low = carry
        target = full_ref[n % 2, n // 8, (n // 2) % 4, K : K + 1, :].astype(jnp.int32)
        member = bin_of == target
        ones = member.astype(F32)
        a = ones.astype(BF)
        ahead = jnp.dot(a, before, preferred_element_type=F32) + base
        rank = jnp.sum(ones * ahead, axis=0, keepdims=True).astype(jnp.int32)
        spot = (row(128, 256) == rank).astype(F32)
        where = jnp.concatenate([(spot * fine).astype(BF), spot.astype(BF)], axis=0)
        got = nt(a, where)
        low = low + got[:, :128]
        high = high + got[:, 128:] * n.astype(F32)
        return base + jnp.sum(ones, axis=1, keepdims=True), high, low

    zero = jnp.zeros((32, 128), F32)
    _, high, low = lax.fori_loop(0, 32, rank_step, (jnp.zeros((32, 1), F32), zero, zero), unroll=8)
    perm_ref[...] = (high * 256.0 + low).astype(jnp.int32)
    down = pltpu.make_async_copy(perm_ref, perm_smem, sem)
    down.start()

    eye = (row(256, 256) == lane(256, 256)).astype(BF)
    blank = jnp.zeros((8, 256), BF)

    def turn_step(n, _):
        at = pl.multiple_of(n * 256, 256)
        both = jnp.concatenate(
            [va_ref[:, :, pl.ds(at, 256)].reshape(120, 256), blank, vb_ref[:, :, pl.ds(at, 256)].reshape(120, 256), blank], axis=0
        )
        rows = nt(eye, both)
        grid_ref[pl.ds(at, 256), 0, :] = rows[:, :128]
        grid_ref[pl.ds(at, 256), 1, :] = rows[:, 128:]
        phase = full_ref[n % 2, n // 8, (n // 2) % 4, :K, :].astype(jnp.int32).astype(F32) * (1.0 / STEP)
        sine, cosine = sin_cos(phase)
        chi, clo = halves(cosine)
        shi, slo = halves(sine)
        rows = nt(eye, jnp.concatenate([chi, shi, clo, slo], axis=0))
        grid_ref[pl.ds(at, 256), 2, :] = rows[:, :128]
        grid_ref[pl.ds(at, 256), 3, :] = rows[:, 128:]
        return 0

    lax.fori_loop(0, 32, turn_step, 0, unroll=2)
    down.wait()

    def move_step(n, _):
        for u in range(16):
            sorted_ref[n * 16 + u] = grid_ref[perm_smem[n // 8, (n % 8) * 16 + u]]
        return 0

    lax.fori_loop(0, OWN // 16, move_step, 0)

    spread = row(128, 128)
    source = jnp.where(spread < 64, spread, spread - 4)
    fits = (spread % 64) < SP
    choose = ((source == lane(128, 128)) & fits).astype(BF)
    upper = row(64, 128) < lane(64, 128) % 64
    first = lane(64, 128) < 64

    def work_step(k, _):
        at = pl.multiple_of(k * 256, 256)
        va = nt(choose, sorted_ref[pl.ds(at, 256), 0, :].astype(BF))
        vb = nt(choose, sorted_ref[pl.ds(at, 256), 1, :].astype(BF))
        table = jnp.concatenate(
            [sorted_ref[pl.ds(at, 256), 2, :].astype(BF), sorted_ref[pl.ds(at, 256), 3, :].astype(BF)], axis=1
        )
        cs_ref[...] = nt(pick_ref[...], table)
        zl, y = k // 4, k % 4
        for c in range(C):
            cosine = cs_ref[c * 128 : c * 128 + 64, :]
            sine = cs_ref[c * 128 + 64 : c * 128 + 128, :]
            parts = []
            for v in (va, vb):
                re, im = v[:64], v[64:]
                turned = jnp.concatenate([re * cosine + im * sine, im * cosine - re * sine], axis=0)
                hi, lo = halves(turned)
                parts.append(jnp.concatenate([hi, lo], axis=0))
            got = []
            for r in range(2):
                w = jnp.concatenate([p[:, r * 128 : (r + 1) * 128] for p in parts], axis=1)
                zz = nt(w, w)
                zz = zz[:128, :128] + zz[:128, 128:] + zz[128:, :128]
                turn = pltpu.roll(zz[64:], 64, 1)
                got.append(zz[:64] + jnp.where(first, turn, -turn))
            d0, d1 = got
            e0, e1 = pltpu.roll(d0, 64, 1), pltpu.roll(d1, 64, 1)
            packed = jnp.where(upper, jnp.where(first, d0, e1), jnp.where(first, e0, d1)).astype(BF)
            xx, zz = c % 4, (c // 4) * 4 + zl
            ax_ref[xx, y, zz] = packed[:32]
            by_ref[y, xx, zz] = packed[32:]
        return 0

    lax.fori_loop(0, 16, work_step, 0)


def local_work(va, vb, full, pick):
    vm = pl.BlockSpec(memory_space=pltpu.VMEM)
    half = jax.ShapeDtypeStruct((4, 4, 8, 32, 128), BF)
    return pl.pallas_call(
        local_kernel,
        out_shape=(half, half),
        in_specs=[vm] * 4,
        out_specs=(vm, vm),
        scratch_shapes=[
            pltpu.VMEM((F, 4, 128), F32),
            pltpu.VMEM((OWN, 4, 128), F32),
            pltpu.VMEM((32, 128), jnp.int32),
            pltpu.SMEM((32, 128), jnp.int32),
            pltpu.VMEM((C * 128, 256), F32),
            pltpu.SemaphoreType.DMA,
        ],
        compiler_params=pltpu.CompilerParams(vmem_limit_bytes=66 * 1000 * 1000),
        name="local_work",
    )(va, vb, full, pick)


def sum_kernel(ax_ref, by_ref, out_ref, ra, rb, s1a, s1b, r2a, r2b, s2, r3, s1_s, s1_r, s2_s, s2_r, s3_s, s3_r):
    x, y, z, core = place()
    x_peers = [device(x + d, y, z, core) for d in (1, 2, 3)]
    y_peers = [device(x, y + d, z, core) for d in (1, 2, 3)]
    z_peers = [device(x, y, z + d, core) for d in range(1, 8)]
    barrier = pltpu.get_barrier_semaphore()
    for peer in x_peers + y_peers + z_peers:
        pl.semaphore_signal(barrier, inc=1, device_id=peer, device_id_type=MESH)
    pl.semaphore_wait(barrier, 13)

    def push(src, dst, send, recv, peer):
        copy = pltpu.make_async_remote_copy(
            src_ref=src, dst_ref=dst, send_sem=send, recv_sem=recv, device_id=peer, device_id_type=MESH
        )
        copy.start()
        return copy

    sides = (
        (0, ax_ref, ra, s1a, r2a, x, y, x_peers, y_peers),
        (1, by_ref, rb, s1b, r2b, y, x, y_peers, x_peers),
    )
    first = []
    for j in range(4):
        for h, src, dst, _, _, p, q, peers, _ in sides:
            part = lax.rem(q + 1 + j, 4)
            for d in range(3):
                to = lax.rem(p + d + 1, 4)
                first.append((h, j, d, push(
                    src.at[to, part], dst.at[d, part], s1_s.at[h, j, d], s1_r.at[h, j, d], peers[d])))
    index = {(h, j, d): copy for h, j, d, copy in first}
    second = []
    for j in range(4):
        for h, src, dst, held, land, p, q, _, peers in sides:
            part = lax.rem(q + 1 + j, 4)
            for d in range(3):
                index[h, j, d].wait_recv()
            total = src[p, part].astype(F32)
            for d in range(3):
                total = total + dst[d, part].astype(F32)
            held[j] = total
            if j < 3:
                second.append((h, j, push(
                    held.at[j], land.at[j], s2_s.at[h, j], s2_r.at[h, j], peers[j])))
    for h, _, _, held, land, *_ in sides:
        for hh, j, copy in second:
            if hh == h:
                copy.wait_recv()
        s2[:, h * 32 : h * 32 + 32, :] = held[3] + land[0] + land[1] + land[2]
    third = []
    for d in range(7):
        to = lax.rem(z + d + 1, 8)
        third.append(push(s2.at[to], r3.at[d], s3_s.at[d], s3_r.at[d], z_peers[d]))
    total = s2[z]
    for d in range(7):
        third[d].wait_recv()
        total = total + r3[d]
    out_ref[...] = total
    for copy in [c for *_, c in first] + [c for *_, c in second] + third:
        copy.wait_send()


def slice_sum(ax, by):
    vm = pl.BlockSpec(memory_space=pltpu.VMEM)
    return pl.pallas_call(
        sum_kernel,
        out_shape=jax.ShapeDtypeStruct((64, 128), F32),
        in_specs=[vm, vm],
        out_specs=vm,
        scratch_shapes=[
            pltpu.VMEM((3, 4, 8, 32, 128), BF),
            pltpu.VMEM((3, 4, 8, 32, 128), BF),
            pltpu.VMEM((4, 8, 32, 128), F32),
            pltpu.VMEM((4, 8, 32, 128), F32),
            pltpu.VMEM((3, 8, 32, 128), F32),
            pltpu.VMEM((3, 8, 32, 128), F32),
            pltpu.VMEM((8, 64, 128), F32),
            pltpu.VMEM((7, 64, 128), F32),
            pltpu.SemaphoreType.DMA((2, 4, 3)),
            pltpu.SemaphoreType.DMA((2, 4, 3)),
            pltpu.SemaphoreType.DMA((2, 3)),
            pltpu.SemaphoreType.DMA((2, 3)),
            pltpu.SemaphoreType.DMA((7,)),
            pltpu.SemaphoreType.DMA((7,)),
        ],
        compiler_params=pltpu.CompilerParams(
            collective_id=1, has_side_effects=True, vmem_limit_bytes=32 * 1000 * 1000
        ),
        name="slice_sum",
    )(ax, by)


def select_kernel(m_ref, pairs_ref, out_ref):
    one, two = pairs_ref[0:1, :], pairs_ref[1:2, :]
    least, most = jnp.minimum(one, two), jnp.maximum(one, two)
    sign = jnp.where(one < two, 1.0, -1.0).astype(F32)
    rows = lax.broadcasted_iota(jnp.int32, (64, 512), 0)
    columns = jnp.concatenate([(rows == 2 * most + p).astype(BF) for p in range(2)]
                              + [(rows == 2 * least + p).astype(BF) for p in range(2)], axis=1)
    m = m_ref[...] * (Q / F)
    m = jnp.concatenate([m[:, :64], m[:, 64:]], axis=0)
    m0 = m.astype(BF)
    rest = m - m0.astype(F32)
    m1 = rest.astype(BF)
    m2 = (rest - m1.astype(F32)).astype(BF)
    got = sum(jnp.dot(part, columns, preferred_element_type=F32) for part in (m0, m1, m2))
    ahead = one < two
    for r in range(2):
        def cell(side, p_row, p_col):
            block = got[r * 64 : r * 64 + 64, (side * 2 + p_col) * 512 : (side * 2 + p_col + 1) * 512]
            station = least if side == 0 else most
            return jnp.sum(jnp.where(rows == 2 * station + p_row, block, 0.0), axis=0, keepdims=True)
        upper = {(a, b): cell(0, a, b) for a in range(2) for b in range(2)}
        lower = {(a, b): cell(1, b, a) for a in range(2) for b in range(2)}
        for p in range(2):
            for p2 in range(2):
                re = jnp.where(ahead, upper[p, p2], upper[p2, p])
                im = sign * jnp.where(ahead, lower[p, p2], lower[p2, p])
                at = r * 8 + p * 2 + p2
                out_ref[at : at + 1, :] = re
                out_ref[at + 4 : at + 5, :] = im


def select(m, pairs):
    return pl.pallas_call(
        select_kernel,
        out_shape=jax.ShapeDtypeStruct((16, 512), F32),
        name="select",
    )(m, pairs)


def on_device(voltage_frequency_samples, lag_lookup_entry, lag_lookup_turning, antenna_pair_members, frequency_bin_target):
    volts = voltage_frequency_samples.reshape(SP, 2, F)
    fixed = jnp.round(lag_lookup_turning * STEP).astype(jnp.int16)
    target = jnp.broadcast_to(frequency_bin_target.astype(jnp.int16)[None, :], (16, F // 32))
    shard = jnp.concatenate([fixed, target], axis=0)

    entry = jnp.repeat(lag_lookup_entry[0], 2, axis=1)
    entry = jnp.pad(entry, ((0, 0), (0, 64 - SP)), constant_values=-1000)
    entry = jnp.stack([entry, entry + K], axis=1).reshape(C * 128, 1)
    pick = (entry == jnp.arange(256, dtype=jnp.int32)[None, :] % 128).astype(BF)

    pairs = jnp.pad(antenna_pair_members.T, ((0, 6), (0, 512 - B)))

    full, other = gather(shard, volts)
    ax, by = local_work(volts, other, full, pick)
    m = slice_sum(ax, by)
    return select(m, pairs)[:, :B].reshape(2, 2, 4, B)


def solution(mesh):
    return jax.shard_map(
        on_device,
        mesh=mesh,
        in_specs=(
            P(None, ("tm", "chan"), None, None, None),
            P("tm", None, None),
            P(None, "chan"),
            P(),
            P("chan"),
        ),
        out_specs=P(("tm", "chan"), None, None, None),
        check_vma=False,
    )
```

time: 539 us -> 130 us (0.24)
  waiting for transfers between devices: 286 us -> 0 us
  local copies, waits for them, and re-layouts: 173 us -> 5.33 us
  Pallas kernels: 0 us -> 121 us
  matrix products: 27.4 us -> 0 us
  other arithmetic: 23.1 us -> 3.23 us
  between operations: 14 us -> 0.09 us
  starting transfers between devices: 9.37 us -> 0 us
    unnamed x2 -> x0, waiting for transfers between devices: 280 us -> none
    pallas_call x0 -> x4, Pallas kernels: none -> 121 us  [the longest x1 64.5 us: local_work(): pl.pallas_call(local_kernel, out_shape=(half, half), in_specs=[vm] * 4, o...]
    unnamed x49 -> x10, local copies, waits for them, and re-layouts: 75.5 us -> 3.06 us
    dot_general x12 -> x0, matrix products: 27.4 us -> none  [the longest x4 20.8 us: correlate(): jnp.einsum('gtaf,gtbf->gabf', left_part, right_part, preferred_element_ty...]
    gather x6 -> x0, local copies, waits for them, and re-layouts: 21.9 us -> none  [the longest x1 8.11 us: on_device(): vis_imag.reshape(full_shape)]
    reshape x3 -> x2, local copies, waits for them, and re-layouts: 23.2 us -> 1.41 us  [the longest x1 1.38 us: on_device(): return select(m, pairs)[:, :B].reshape(2, 2, 4, B)]
    cos x1 -> x0, other arithmetic: 13.8 us -> none  [on_device(): cosine = jnp.cos(phase_diff)]
    another operation x3 -> x1, local copies, waits for them, and re-layouts: 13.8 us -> 0.07 us  [on_device(): entry = jnp.stack([entry, entry + K], axis=1).reshape(C * 128, 1)]
  transfers between devices with their start and end apart: 2 -> 0, of which waited for: 2 -> 0; matrix products, arithmetic and copies ran while one was open for 7% -> 0% of each run, Pallas kernels for 0% -> 0%
where the time goes in v1:
time: 130 us; the launch traced here: 129 us
  Pallas kernels  121 us (93%)
  local copies, waits for them, and re-layouts  5.33 us (4%)
  other arithmetic  3.23 us (2%)
    pallas_call x1, Pallas kernels, local_work(): pl.pallas_call(local_kernel, out_shape=(half, half), in_specs=[vm] * 4, o...  64.5 us
    pallas_call x1, Pallas kernels, slice_sum(): pl.pallas_call(sum_kernel, out_shape=jax.ShapeDtypeStruct((64, 128), F32)...  33.6 us
    pallas_call x1, Pallas kernels, gather(): pl.pallas_call(gather_kernel, out_shape=(jax.ShapeDtypeStruct((2, 4, 4) +...  20.6 us
    unnamed x10, local copies, waits for them, and re-layouts  3.06 us

profile of v1, /device:TPU:24, one launch (start us, length us, event | category | flops | bytes accessed | tf_op | source)
XLA Modules:
  0.0 129.4 jit_solution(10767623301643443080)
XLA Ops:
  0.0 0.0 copy-start.3
  0.0 0.9 round-nearest-even_convert_fusion
  0.9 0.7 convert_element_type.10
  1.6 0.6 pad_add_fusion.1.sh_ref
  2.2 20.6 %gather.1 = (s16[2,4,4,80,256]{4,3,2,1,0:T(8,128)(2,1)}, bf16[60,2,8192]{2,1,0:T(2,128)(2,1)}) custom-call(s16[80,256]{1,0:T(8,128)(2,1)} %pad_add_fusion.1.sh_ref, bf16[60,2,8192]{2,1,0:T(2,128)(2,1)} %bitcast.10), custom_call_target="tpu_custom_call" | custom-call | tf_op jit(solution)/shard_map/gather/pallas_call | solution.py:111
  22.8 0.0 copy-done.3
  22.8 0.1 copy.12
  23.0 0.1 copy.13
  23.0 0.1 eq.17
  23.1 1.0 compare_convert_fusion.pick_ref
  24.2 0.0 copy-start.4
  24.2 64.5 %local_work.1 = (bf16[4,4,8,32,128]{4,3,2,1,0:T(8,128)(2,1)}, bf16[4,4,8,32,128]{4,3,2,1,0:T(8,128)(2,1)}) custom-call(bf16[60,2,8192]{2,1,0:T(2,128)(2,1)} %bitcast.11, bf16[60,2,8192]{2,1,0:T(2,128)(2,1)} %get-tuple-element.9.vb_ref, s16[2,4,4,80,256]{4,3,2,1,0:T(8,128)(2,1)} %get-tuple-element.10.full_ref, bf16[1024,256]{1,0:T(8,128)(2,1)} %compare_convert_fusion.pick_ref), custom_call_target="tpu_custom_call" | custom-call | tf_op jit(solution)/shard_map/local_work/pallas_call | solution.py:256
  88.7 0.0 copy-start
  88.7 1.2 copy-done
  89.9 0.0 copy-start.1
  89.9 1.2 copy-done.1
  91.1 33.6 %slice_sum.1.m_ref = f32[64,128]{1,0:T(8,128)S(1)} custom-call(bf16[4,4,8,32,128]{4,3,2,1,0:T(8,128)(2,1)S(1)} %copy-done, bf16[4,4,8,32,128]{4,3,2,1,0:T(8,128)(2,1)S(1)} %copy-done.1), custom_call_target="tpu_custom_call" | custom-call | tf_op jit(solution)/shard_map/slice_sum/pallas_call | solution.py:337
  124.7 0.0 copy-start.2
  124.7 0.6 copy-done.2
  125.3 0.0 copy-done.4
  125.3 0.6 pad.9.pairs_ref
  125.9 2.1 %select.5 = f32[16,512]{1,0:T(8,128)} custom-call(f32[64,128]{1,0:T(8,128)} %copy-done.2, s32[8,512]{1,0:T(8,128)} %pad.9.pairs_ref), custom_call_target="tpu_custom_call" | custom-call | tf_op jit(solution)/shard_map/select/pallas_call | solution.py:397
  128.0 1.4 %reshape.29 = f32[2,2,4,435]{3,2,1,0:T(4,128)} reshape(f32[16,435]{1,0:T(8,128)} %bitcast.12) | data formatting | bytes 55680 | tf_op jit(solution)/shard_map/reshape | solution.py:420
  (6 shorter events, 0.1 us)
Async XLA Ops:
  0.0 22.8 %copy-start.3 = (s32[1,8,30]{2,1,0:T(8,128)S(1)}, s32[1,8,30]{2,1,0:T(8,128)}, u32[]{:S(2)}) copy-start(s32[1,8,30]{2,1,0:T(8,128)} %param.6) | copy-start | bytes 2884
  24.2 101.2 %copy-start.4 = (s32[435,2]{0,1:T(2,128)S(1)}, s32[435,2]{0,1:T(2,128)}, u32[]{:S(2)}) copy-start(s32[435,2]{0,1:T(2,128)} %param.8) | copy-start | bytes 10444
  88.7 1.2 copy-start
  89.9 1.2 copy-start.1
  124.7 0.6 copy-start.2

commit v2 on v1

--- a/solution.py
+++ b/solution.py
@@ -146,7 +146,16 @@
     return hi, (value - hi.astype(F32)).astype(BF)
 
 
-def local_kernel(va_ref, vb_ref, full_ref, pick_ref, ax_ref, by_ref, grid_ref, sorted_ref, perm_ref, perm_smem, cs_ref, sem):
+def local_kernel(va_hbm, vb_hbm, full_ref, pick_ref, ax_ref, by_ref, grid_ref, s0_ref, s1_ref, perm_ref, perm_smem, cs_ref, va_ref, vb_ref, sem, load_sem):
+
+    def load(part, side):
+        here = (slice(None), slice(None), pl.ds(pl.multiple_of(part * 2048, 2048), 2048))
+        src, dst = ((va_hbm, va_ref), (vb_hbm, vb_ref))[side]
+        return pltpu.make_async_copy(src.at[here], dst.at[here], load_sem.at[side, part])
+
+    for part in range(4):
+        load(part, 0).start()
+        load(part, 1).start()
     core = lax.axis_index("chan") % 2
     lane = lambda r, c: lax.broadcasted_iota(jnp.int32, (r, c), 1)
     row = lambda r, c: lax.broadcasted_iota(jnp.int32, (r, c), 0)
@@ -172,10 +181,6 @@
         return base + jnp.sum(ones, axis=1, keepdims=True), high, low
 
     zero = jnp.zeros((32, 128), F32)
-    _, high, low = lax.fori_loop(0, 32, rank_step, (jnp.zeros((32, 1), F32), zero, zero), unroll=8)
-    perm_ref[...] = (high * 256.0 + low).astype(jnp.int32)
-    down = pltpu.make_async_copy(perm_ref, perm_smem, sem)
-    down.start()
 
     eye = (row(256, 256) == lane(256, 256)).astype(BF)
     blank = jnp.zeros((8, 256), BF)
@@ -197,15 +202,30 @@
         grid_ref[pl.ds(at, 256), 3, :] = rows[:, 128:]
         return 0
 
-    lax.fori_loop(0, 32, turn_step, 0, unroll=2)
+    def both_steps(n, carry):
+        turn_step(n, 0)
+        return rank_step(n, carry)
+
+    def part_step(part, carry):
+        load(part, 0).wait()
+        load(part, 1).wait()
+        return lax.fori_loop(0, 8, lambda n, held: both_steps(part * 8 + n, held), carry, unroll=8)
+
+    _, high, low = lax.fori_loop(0, 4, part_step, (jnp.zeros((32, 1), F32), zero, zero))
+    perm_ref[...] = (high * 256.0 + low).astype(jnp.int32)
+    down = pltpu.make_async_copy(perm_ref, perm_smem, sem)
+    down.start()
     down.wait()
+
+    def move(dst, group, u):
+        dst[u] = grid_ref[perm_smem[2 * group + u // 128, u % 128]]
 
     def move_step(n, _):
         for u in range(16):
-            sorted_ref[n * 16 + u] = grid_ref[perm_smem[n // 8, (n % 8) * 16 + u]]
+            s0_ref[n * 16 + u] = grid_ref[perm_smem[n // 8, (n % 8) * 16 + u]]
         return 0
 
-    lax.fori_loop(0, OWN // 16, move_step, 0)
+    lax.fori_loop(0, 16, move_step, 0)
 
     spread = row(128, 128)
     source = jnp.where(spread < 64, spread, spread - 4)
@@ -214,16 +234,16 @@
     upper = row(64, 128) < lane(64, 128) % 64
     first = lane(64, 128) < 64
 
-    def work_step(k, _):
-        at = pl.multiple_of(k * 256, 256)
-        va = nt(choose, sorted_ref[pl.ds(at, 256), 0, :].astype(BF))
-        vb = nt(choose, sorted_ref[pl.ds(at, 256), 1, :].astype(BF))
-        table = jnp.concatenate(
-            [sorted_ref[pl.ds(at, 256), 2, :].astype(BF), sorted_ref[pl.ds(at, 256), 3, :].astype(BF)], axis=1
-        )
+    def work(k, src, dst):
+        ahead = jnp.minimum(k + 1, 15)
+        va = nt(choose, src[:, 0, :].astype(BF))
+        vb = nt(choose, src[:, 1, :].astype(BF))
+        table = jnp.concatenate([src[:, 2, :].astype(BF), src[:, 3, :].astype(BF)], axis=1)
         cs_ref[...] = nt(pick_ref[...], table)
         zl, y = k // 4, k % 4
         for c in range(C):
+            for u in range(32):
+                move(dst, ahead, c * 32 + u)
             cosine = cs_ref[c * 128 : c * 128 + 64, :]
             sine = cs_ref[c * 128 + 64 : c * 128 + 128, :]
             parts = []
@@ -245,34 +265,49 @@
             xx, zz = c % 4, (c // 4) * 4 + zl
             ax_ref[xx, y, zz] = packed[:32]
             by_ref[y, xx, zz] = packed[32:]
+
+    def work_step(n, _):
+        work(2 * n, s0_ref, s1_ref)
+        work(2 * n + 1, s1_ref, s0_ref)
         return 0
 
-    lax.fori_loop(0, 16, work_step, 0)
+    lax.fori_loop(0, 8, work_step, 0)
 
 
 def local_work(va, vb, full, pick):
     vm = pl.BlockSpec(memory_space=pltpu.VMEM)
+    hbm = pl.BlockSpec(memory_space=pl.ANY)
     half = jax.ShapeDtypeStruct((4, 4, 8, 32, 128), BF)
     return pl.pallas_call(
         local_kernel,
         out_shape=(half, half),
-        in_specs=[vm] * 4,
+        in_specs=[hbm, hbm, vm, vm],
         out_specs=(vm, vm),
         scratch_shapes=[
             pltpu.VMEM((F, 4, 128), F32),
-            pltpu.VMEM((OWN, 4, 128), F32),
+            pltpu.VMEM((256, 4, 128), F32),
+            pltpu.VMEM((256, 4, 128), F32),
             pltpu.VMEM((32, 128), jnp.int32),
             pltpu.SMEM((32, 128), jnp.int32),
             pltpu.VMEM((C * 128, 256), F32),
+            pltpu.VMEM((SP, 2, F), BF),
+            pltpu.VMEM((SP, 2, F), BF),
             pltpu.SemaphoreType.DMA,
+            pltpu.SemaphoreType.DMA((2, 4)),
         ],
         compiler_params=pltpu.CompilerParams(vmem_limit_bytes=66 * 1000 * 1000),
         name="local_work",
     )(va, vb, full, pick)
 
 
-def sum_kernel(ax_ref, by_ref, out_ref, ra, rb, s1a, s1b, r2a, r2b, s2, r3, s1_s, s1_r, s2_s, s2_r, s3_s, s3_r):
+def sum_kernel(ax_ref, by_ref, out_ref, own_a, own_b, ra, rb, s1a, s1b, r2a, r2b, s2, r3, s1_s, s1_r, s2_s, s2_r, s3_s, s3_r, own_sem):
     x, y, z, core = place()
+    mine = [
+        pltpu.make_async_copy(ax_ref.at[x], own_a, own_sem.at[0]),
+        pltpu.make_async_copy(by_ref.at[y], own_b, own_sem.at[1]),
+    ]
+    for copy in mine:
+        copy.start()
     x_peers = [device(x + d, y, z, core) for d in (1, 2, 3)]
     y_peers = [device(x, y + d, z, core) for d in (1, 2, 3)]
     z_peers = [device(x, y, z + d, core) for d in range(1, 8)]
@@ -301,13 +336,15 @@
                 first.append((h, j, d, push(
                     src.at[to, part], dst.at[d, part], s1_s.at[h, j, d], s1_r.at[h, j, d], peers[d])))
     index = {(h, j, d): copy for h, j, d, copy in first}
+    for copy in mine:
+        copy.wait()
     second = []
     for j in range(4):
         for h, src, dst, held, land, p, q, _, peers in sides:
             part = lax.rem(q + 1 + j, 4)
             for d in range(3):
                 index[h, j, d].wait_recv()
-            total = src[p, part].astype(F32)
+            total = (own_a, own_b)[h][part].astype(F32)
             for d in range(3):
                 total = total + dst[d, part].astype(F32)
             held[j] = total
@@ -337,9 +374,11 @@
     return pl.pallas_call(
         sum_kernel,
         out_shape=jax.ShapeDtypeStruct((64, 128), F32),
-        in_specs=[vm, vm],
+        in_specs=[pl.BlockSpec(memory_space=pl.ANY)] * 2,
         out_specs=vm,
         scratch_shapes=[
+            pltpu.VMEM((4, 8, 32, 128), BF),
+            pltpu.VMEM((4, 8, 32, 128), BF),
             pltpu.VMEM((3, 4, 8, 32, 128), BF),
             pltpu.VMEM((3, 4, 8, 32, 128), BF),
             pltpu.VMEM((4, 8, 32, 128), F32),
@@ -354,6 +393,7 @@
             pltpu.SemaphoreType.DMA((2, 3)),
             pltpu.SemaphoreType.DMA((7,)),
             pltpu.SemaphoreType.DMA((7,)),
+            pltpu.SemaphoreType.DMA((2,)),
         ],
         compiler_params=pltpu.CompilerParams(
             collective_id=1, has_side_effects=True, vmem_limit_bytes=32 * 1000 * 1000

time: 130 us -> 113 us (0.87)
  Pallas kernels: 121 us -> 104 us
    pallas_call x1, Pallas kernels: 64.5 us -> 47.7 us  [local_work(): pl.pallas_call(local_kernel, out_shape=(half, half), in_specs=[hbm, hbm,...]
where the time goes in v2:
time: 113 us
  Pallas kernels  104 us (92%)
  local copies, waits for them, and re-layouts  5.33 us (5%)
  other arithmetic  3.23 us (3%)
    pallas_call x1, Pallas kernels, local_work(): pl.pallas_call(local_kernel, out_shape=(half, half), in_specs=[hbm, hbm,...  47.7 us
    pallas_call x1, Pallas kernels, slice_sum(): pl.pallas_call(sum_kernel, out_shape=jax.ShapeDtypeStruct((64, 128), F32)...  33.7 us
    pallas_call x1, Pallas kernels, gather(): pl.pallas_call(gather_kernel, out_shape=(jax.ShapeDtypeStruct((2, 4, 4) +...  20.6 us
    unnamed x10, local copies, waits for them, and re-layouts  3.06 us

profile of v2, /device:TPU:24, one launch (start us, length us, event | category | flops | bytes accessed | tf_op | source)
XLA Modules:
  0.0 112.8 jit_solution(4494886064567123621)
XLA Ops:
  0.0 0.0 copy-start.3
  0.0 0.9 round-nearest-even_convert_fusion
  0.9 0.7 convert_element_type.10
  1.6 0.6 pad_add_fusion.1.sh_ref
  2.2 20.6 %gather.1 = (s16[2,4,4,80,256]{4,3,2,1,0:T(8,128)(2,1)}, bf16[60,2,8192]{2,1,0:T(2,128)(2,1)}) custom-call(s16[80,256]{1,0:T(8,128)(2,1)} %pad_add_fusion.1.sh_ref, bf16[60,2,8192]{2,1,0:T(2,128)(2,1)} %bitcast.10), custom_call_target="tpu_custom_call" | custom-call | tf_op jit(solution)/shard_map/gather/pallas_call | solution.py:111
  22.8 0.0 copy-done.3
  22.8 0.1 copy.12
  23.0 0.1 copy.13
  23.0 0.1 eq.17
  23.1 1.0 compare_convert_fusion.pick_ref
  24.2 0.0 copy-start.4
  24.2 47.7 %local_work.1 = (bf16[4,4,8,32,128]{4,3,2,1,0:T(8,128)(2,1)}, bf16[4,4,8,32,128]{4,3,2,1,0:T(8,128)(2,1)}) custom-call(bf16[60,2,8192]{2,1,0:T(2,128)(2,1)} %bitcast.11, bf16[60,2,8192]{2,1,0:T(2,128)(2,1)} %get-tuple-element.9.vb_hbm, s16[2,4,4,80,256]{4,3,2,1,0:T(8,128)(2,1)} %get-tuple-element.10.full_ref, bf16[1024,256]{1,0:T(8,128)(2,1)} %compare_convert_fusion.pick_ref), custom_call_target="tpu_custom_call" | custom-call | tf_op jit(solution)/shard_map/local_work/pallas_call | solution.py:281
  71.9 0.0 copy-start
  71.9 1.2 %copy-done = bf16[4,4,8,32,128]{4,3,2,1,0:T(8,128)(2,1)S(1)} copy-done((bf16[4,4,8,32,128]{4,3,2,1,0:T(8,128)(2,1)S(1)}, bf16[4,4,8,32,128]{4,3,2,1,0:T(8,128)(2,1)}, u32[]{:S(2)}) %copy-start) | copy-done | bytes 1048600
  73.1 0.0 copy-start.1
  73.1 1.2 %copy-done.1 = bf16[4,4,8,32,128]{4,3,2,1,0:T(8,128)(2,1)S(1)} copy-done((bf16[4,4,8,32,128]{4,3,2,1,0:T(8,128)(2,1)S(1)}, bf16[4,4,8,32,128]{4,3,2,1,0:T(8,128)(2,1)}, u32[]{:S(2)}) %copy-start.1) | copy-done | bytes 1048600
  74.3 33.7 %slice_sum.1.m_ref = f32[64,128]{1,0:T(8,128)S(1)} custom-call(bf16[4,4,8,32,128]{4,3,2,1,0:T(8,128)(2,1)S(1)} %copy-done, bf16[4,4,8,32,128]{4,3,2,1,0:T(8,128)(2,1)S(1)} %copy-done.1), custom_call_target="tpu_custom_call" | custom-call | tf_op jit(solution)/shard_map/slice_sum/pallas_call | solution.py:374
  108.1 0.0 copy-start.2
  108.1 0.6 copy-done.2
  108.7 0.0 copy-done.4
  108.7 0.6 pad.9.pairs_ref
  109.3 2.1 %select.5 = f32[16,512]{1,0:T(8,128)} custom-call(f32[64,128]{1,0:T(8,128)} %copy-done.2, s32[8,512]{1,0:T(8,128)} %pad.9.pairs_ref), custom_call_target="tpu_custom_call" | custom-call | tf_op jit(solution)/shard_map/select/pallas_call | solution.py:437
  111.4 1.4 %reshape.29 = f32[2,2,4,435]{3,2,1,0:T(4,128)} reshape(f32[16,435]{1,0:T(8,128)} %bitcast.12) | data formatting | bytes 55680 | tf_op jit(solution)/shard_map/reshape | solution.py:460
  (6 shorter events, 0.1 us)
Async XLA Ops:
  0.0 22.8 %copy-start.3 = (s32[1,8,30]{2,1,0:T(8,128)S(1)}, s32[1,8,30]{2,1,0:T(8,128)}, u32[]{:S(2)}) copy-start(s32[1,8,30]{2,1,0:T(8,128)} %param.6) | copy-start | bytes 2884
  24.2 84.6 %copy-start.4 = (s32[435,2]{0,1:T(2,128)S(1)}, s32[435,2]{0,1:T(2,128)}, u32[]{:S(2)}) copy-start(s32[435,2]{0,1:T(2,128)} %param.8) | copy-start | bytes 10444
  71.9 1.2 %copy-start = (bf16[4,4,8,32,128]{4,3,2,1,0:T(8,128)(2,1)S(1)}, bf16[4,4,8,32,128]{4,3,2,1,0:T(8,128)(2,1)}, u32[]{:S(2)}) copy-start(bf16[4,4,8,32,128]{4,3,2,1,0:T(8,128)(2,1)} %get-tuple-element.11.ax_ref) | copy-start | bytes 3145732
  73.1 1.2 %copy-start.1 = (bf16[4,4,8,32,128]{4,3,2,1,0:T(8,128)(2,1)S(1)}, bf16[4,4,8,32,128]{4,3,2,1,0:T(8,128)(2,1)}, u32[]{:S(2)}) copy-start(bf16[4,4,8,32,128]{4,3,2,1,0:T(8,128)(2,1)} %get-tuple-element.12.by_ref) | copy-start | bytes 3145732
  108.1 0.6 copy-start.2
